TPU v7x, 256 devices: a whole 4x4x8 slice. The times are simulated.
256 devices in a mesh: pipe: 16 (over z, core), tensor: 16 (over y, x).
Axes of the slice: x: 4, y: 4, z: 8, core: 2. Of those that a mesh axis runs over, the one named last changes fastest.
Arguments:
- handed_acts: bfloat16 [16, 256, 12288], P('pipe', None, 'tensor'), may hold values from -6 to 6
- handed_grads: bfloat16 [16, 256, 12288], P('pipe', None, 'tensor'), may hold values from -6 to 6
- saved_inputs: bfloat16 [16, 256, 12288], P('pipe', None, 'tensor'), may hold values from -6 to 6
- embedded: bfloat16 [256, 12288], P(None, 'tensor'), may hold values from -6 to 6
- loss_grad: bfloat16 [256, 12288], P(None, 'tensor'), may hold values from -6 to 6
- w_in: bfloat16 [16, 96, 3, 256, 256], P('pipe', 'tensor'), may hold values from -0.21875 to 0.21875
- w_out: bfloat16 [16, 96, 3, 256, 256], P('pipe', 'tensor'), may hold values from -0.15625 to 0.15625
- cols_in: int32 [96, 3], P('tensor'), may hold values from 0 to 2
- cols_out: int32 [96, 3], P('tensor'), may hold values from 0 to 2
Outputs:
- out_acts: bfloat16 [16, 256, 12288], P('pipe', None, 'tensor')
- in_grads: bfloat16 [16, 256, 12288], P('pipe', None, 'tensor')
- grad_w_in: bfloat16 [16, 96, 3, 256, 256], P('pipe', 'tensor')
- grad_w_out: bfloat16 [16, 96, 3, 256, 256], P('pipe', 'tensor')
All inputs are finite; a program needn't handle non-finite values.
Results may differ from a plain program's by a relative error of at most 0.0049.
Values may be sent and summed in bfloat16 or wider, within the bound.
No kernel may reach another device: no remote copies, remote signals or barrier semaphores. Data moves between devices by JAX's collectives and lax.ppermute only.
A program may use at most 128 MiB of HBM per device.

v0:
```python
import functools

import jax
import jax.numpy as jnp
from jax import lax
from jax.experimental import pallas as pl
from jax.experimental.pallas import tpu as pltpu
from jax.sharding import PartitionSpec as P


BF = jnp.bfloat16
F32 = jnp.float32
ROOT = 0.7978845608028654
CUBE = 0.044715


def dot(a, b, dims):
    return lax.dot_general(a, b, (dims, ((), ())), preferred_element_type=F32)


NN = ((1,), (0,))
NT = ((1,), (1,))
TN = ((0,), (0,))


def gelu(v):
    return 0.5 * v * (1.0 + jnp.tanh(ROOT * (v + CUBE * v * v * v)))


def gelu_and_slope(v):
    square = v * v
    t = jnp.tanh(ROOT * (v + CUBE * v * square))
    half = 0.5 * (1.0 + t)
    slope = half + 0.5 * v * (1.0 - t * t) * (ROOT * (1.0 + 3.0 * CUBE * square))
    return v * half, slope


def column(table, h, k, size):
    return pl.ds(pl.multiple_of(table[k, h] * size, size), size)


def picked(table, h, slots, size):
    return jnp.concatenate(
        [ref[:, column(table, h, k, size)] for k, ref in enumerate(slots)], axis=1
    )


def forward_kernel(cin, cout, x0, x1, x2, w_in, w_out, own, c1, c2, acc):
    hidden, slots, size, _ = w_in.shape
    own[...] = x0[...].astype(F32)
    acc[...] = jnp.zeros_like(acc)
    sums = (own, acc.at[0], acc.at[1])
    for h in range(hidden):
        x = picked(cin, h, (x0, x1, x2), size)
        pre = dot(x, w_in[h].reshape(slots * size, size), NN)
        hid = gelu(pre).astype(BF)
        for k in range(slots):
            sums[k][:, column(cout, h, k, size)] += dot(hid, w_out[h, k], NN)
    c1[...] = acc[0].astype(BF)
    c2[...] = acc[1].astype(BF)


def hidden_kernel(cin, x0, x1, x2, w_in, hid, slope):
    hidden, slots, size, _ = w_in.shape
    for h in range(hidden):
        x = picked(cin, h, (x0, x1, x2), size)
        pre = dot(x, w_in[h].reshape(slots * size, size), NN)
        value, rate = gelu_and_slope(pre)
        hid[:, h * size : (h + 1) * size] = value.astype(BF)
        slope[:, h * size : (h + 1) * size] = rate


def backward_kernel(cin, cout, g0, g1, g2, slope, w_in, w_out, own, c1, c2, dpre, acc):
    hidden, slots, size, _ = w_in.shape
    own[...] = g0[...].astype(F32)
    acc[...] = jnp.zeros_like(acc)
    sums = (own, acc.at[0], acc.at[1])
    for h in range(hidden):
        dhid = None
        for k, ref in enumerate((g0, g1, g2)):
            term = dot(ref[:, column(cout, h, k, size)], w_out[h, k], NT)
            dhid = term if dhid is None else dhid + term
        grad = (dhid * slope[:, h * size : (h + 1) * size]).astype(BF)
        dpre[:, h * size : (h + 1) * size] = grad
        for k in range(slots):
            sums[k][:, column(cin, h, k, size)] += dot(grad, w_in[h, k], NT)
    c1[...] = acc[0].astype(BF)
    c2[...] = acc[1].astype(BF)


def weights_kernel(
    cin, cout, x0, x1, x2, g0, g1, g2, hid, dpre, gw_in, gw_out, buf_in, buf_out, sems
):
    hidden, _, size, _ = buf_in.shape
    copies = []
    for h in range(hidden):
        span = slice(h * size, (h + 1) * size)
        for k, (x, g) in enumerate(((x0, g0), (x1, g1), (x2, g2))):
            buf_out[h, k] = dot(hid[:, span], g[:, column(cout, h, k, size)], TN).astype(BF)
            buf_in[h, k] = dot(x[:, column(cin, h, k, size)], dpre[:, span], TN).astype(BF)
        for i, (src, dst) in enumerate(((buf_in, gw_in), (buf_out, gw_out))):
            copy = pltpu.make_async_copy(src.at[h], dst.at[h], sems.at[i, h])
            copy.start()
            copies.append(copy)
    for copy in copies:
        copy.wait()


VMEM = pl.BlockSpec(memory_space=pltpu.VMEM)
SMEM = pl.BlockSpec(memory_space=pltpu.SMEM)
HBM = pl.BlockSpec(memory_space=pltpu.HBM)


def in_hbm(*arrays):
    return [pltpu.with_memory_space_constraint(x, pltpu.HBM) for x in arrays]


def pick_kernel(
    sections, handed_a, first_a, handed_g, last_g, saved, cin, cout,
    acts, grads, kept, cin_v, cout_v, sems,
):
    section = lax.axis_index("pipe")
    ends = ((sections - 1, first_a, handed_a, acts), (0, last_g, handed_g, grads))
    fixed = ((cin, cin_v), (cout, cout_v), (saved, kept))
    copies = [pltpu.make_async_copy(*pair, sems.at[i]) for i, pair in enumerate(fixed)]

    def each(act):
        for i, (end, own, handed, out) in enumerate(ends):
            for src, hit in ((own, section == end), (handed, section != end)):

                @pl.when(hit)
                def _(src=src, out=out, i=i):
                    act(pltpu.make_async_copy(src, out, sems.at[len(fixed) + i]))

    each(lambda copy: copy.start())
    for copy in copies:
        copy.start()
    each(lambda copy: copy.wait())
    for copy in copies:
        copy.wait()


def pick(handed_a, first_a, handed_g, last_g, saved, cin, cout):
    act = jax.ShapeDtypeStruct(saved.shape, saved.dtype)
    table = jax.ShapeDtypeStruct(cin.shape, cin.dtype)
    return pl.pallas_call(
        functools.partial(pick_kernel, lax.axis_size("pipe")),
        in_specs=[HBM] * 7,
        out_specs=(VMEM,) * 5,
        scratch_shapes=[pltpu.SemaphoreType.DMA((5,))],
        out_shape=(act, act, act, table, table),
        cost_estimate=pl.CostEstimate(
            flops=0, bytes_accessed=6 * saved.size * saved.dtype.itemsize, transcendentals=0
        ),
        compiler_params=pltpu.CompilerParams(vmem_limit_bytes=4 << 20),
        name="pick",
    )(*in_hbm(handed_a, first_a, handed_g, last_g, saved, cin, cout))


def stage_kernel(w_in, w_out, w_in_v, w_out_v, sems):
    copies = [
        pltpu.make_async_copy(src.at[h], dst.at[h], sems.at[i, h])
        for i, (src, dst) in enumerate(((w_in, w_in_v), (w_out, w_out_v)))
        for h in range(src.shape[0])
    ]
    for copy in copies:
        copy.start()
    for copy in copies:
        copy.wait()


def stage(w_in, w_out):
    weight = jax.ShapeDtypeStruct(w_in.shape, w_in.dtype)
    return pl.pallas_call(
        stage_kernel,
        in_specs=[HBM] * 2,
        out_specs=(VMEM,) * 2,
        scratch_shapes=[pltpu.SemaphoreType.DMA((2, w_in.shape[0]))],
        out_shape=(weight, weight),
        cost_estimate=pl.CostEstimate(
            flops=0, bytes_accessed=4 * w_in.size * w_in.dtype.itemsize, transcendentals=0
        ),
        compiler_params=pltpu.CompilerParams(vmem_limit_bytes=8 << 20),
        name="stage",
    )(*in_hbm(w_in, w_out))


def run(body, tables, ins, outs, out_spec, scratch, flops):
    size = sum(x.size * x.dtype.itemsize for x in ins) + sum(
        x.size * jnp.dtype(x.dtype).itemsize for x in outs
    )
    return pl.pallas_call(
        body,
        in_specs=[SMEM] * len(tables) + [VMEM] * len(ins),
        out_specs=(out_spec,) * len(outs),
        scratch_shapes=scratch,
        out_shape=outs,
        cost_estimate=pl.CostEstimate(flops=flops, bytes_accessed=size, transcendentals=0),
        compiler_params=pltpu.CompilerParams(vmem_limit_bytes=16 << 20),
    )(*tables, *ins)


def shards(
    handed_acts, handed_grads, saved_inputs, embedded, loss_grad, w_in, w_out, cols_in, cols_out
):
    tokens, width = embedded.shape
    w_in, w_out = w_in[0], w_out[0]
    hidden, slots, size, _ = w_in.shape
    sections = lax.axis_size("pipe")
    group = lax.axis_size("tensor")
    masks = (0, 1, group // 2)

    def send(value, step, mask):
        route = [
            (s * group + t, (s + step) % sections * group + (t ^ mask))
            for s in range(sections)
            for t in range(group)
        ]
        return lax.ppermute(value, ("pipe", "tensor"), route)

    def exchange(values, step=0):
        got = []
        for k in (1, 2):
            value = values[k - 1] if isinstance(values, tuple) else values
            got.append(send(value, step, masks[k]))
        return got

    saved = saved_inputs[0]
    xb = [saved] + exchange(saved)
    acts, grads, kept, cin, cout = pick(
        handed_acts[0], embedded, handed_grads[0], loss_grad, saved, cols_in.T, cols_out.T
    )
    xb[0] = kept
    far = exchange(acts, step=1)
    xa = [send(acts, 1, 0)] + far
    grads = send(grads, -1, 0)
    w_in, w_out = stage(w_in, w_out)
    gb = [grads] + exchange(grads)

    act = jax.ShapeDtypeStruct((tokens, width), BF)
    total = jax.ShapeDtypeStruct((tokens, width), F32)
    hid_bf = jax.ShapeDtypeStruct((tokens, hidden * size), BF)
    hid_f32 = jax.ShapeDtypeStruct((tokens, hidden * size), F32)
    weight = jax.ShapeDtypeStruct(w_in.shape, BF)
    acc = pltpu.VMEM((slots - 1, tokens, width), F32)
    unit = 2 * tokens * size * size * hidden * slots

    hid_b, slope_b = run(hidden_kernel, (cin,), (*xb, w_in), (hid_bf, hid_f32), VMEM, [], unit)
    own_a, a1, a2 = run(
        forward_kernel, (cin, cout), (*xa, w_in, w_out), (total, act, act), VMEM, [acc],
        2 * unit,
    )
    a1, a2 = exchange((a1, a2))
    own_b, b1, b2, dpre = run(
        backward_kernel, (cin, cout), (*gb, slope_b, w_in, w_out), (total, act, act, hid_bf),
        VMEM, [acc], 2 * unit,
    )
    b1, b2 = exchange((b1, b2))
    held = pltpu.VMEM(w_in.shape, BF)
    gw_in, gw_out = run(
        weights_kernel, (cin, cout), (*xb, *gb, hid_b, dpre), (weight, weight), HBM,
        [held, held, pltpu.SemaphoreType.DMA((2, hidden))], 2 * unit,
    )
    out_acts = (own_a + a1.astype(F32) + a2.astype(F32)).astype(BF)
    in_grads = (own_b + b1.astype(F32) + b2.astype(F32)).astype(BF)
    return (out_acts[None], in_grads[None], gw_in[None], gw_out[None])


def solution(mesh):
    in_specs = (
        P("pipe", None, "tensor"),
        P("pipe", None, "tensor"),
        P("pipe", None, "tensor"),
        P(None, "tensor"),
        P(None, "tensor"),
        P("pipe", "tensor", None, None, None),
        P("pipe", "tensor", None, None, None),
        P("tensor", None),
        P("tensor", None),
    )
    out_specs = (
        P("pipe", None, "tensor"),
        P("pipe", None, "tensor"),
        P("pipe", "tensor", None, None, None),
        P("pipe", "tensor", None, None, None),
    )
    return jax.shard_map(shards, mesh=mesh, in_specs=in_specs, out_specs=out_specs, check_vma=False)
```

profile of v0, /device:TPU:2, one launch (start us, length us, event | category | flops | bytes accessed | tf_op | source)
XLA Modules:
  0.0 55.0 jit_solution(5253948275368103841)
XLA Ops:
  0.6 1.3 %pick.1 = (bf16[256,768]{1,0:T(8,128)(2,1)S(1)}, bf16[256,768]{1,0:T(8,128)(2,1)S(1)}, bf16[256,768]{1,0:T(8,128)(2,1)S(1)}, s32[3,6]{1,0:T(4,128)S(1)}, s32[3,6]{1,0:T(4,128)S(1)}) custom-call(bf16[256,768]{1,0:T(8,128)(2,1)} %bitcast.15, bf16[256,768]{1,0:T(8,128)(2,1)} %first_a.1, bf16[256,768]{1,0:T(8,128)(2,1)} %bitcast.16, bf16[256,768]{1,0:T(8,128)(2,1)} %last_g.1, ...), custom_call_target="tpu_custom_call" | custom-call | bytes 2359296 | tf_op jit(solution)/shard_map/pick/pallas_call | solution.py:146
  2.0 5.3 %collective-permute-start.5 = (bf16[256,768]{1,0:T(8,128)(2,1)S(1)}, bf16[256,768]{1,0:T(8,128)(2,1)S(1)}, u32[]{:S(2)}, u32[]{:S(2)}) collective-permute-start(bf16[256,768]{1,0:T(8,128)(2,1)S(1)} %get-tuple-element.30), channel_id=1, source_target_pairs={{0,240},{1,241},{2,242},{3,243},{4,244},{5,245},{6,246},{7,247},{8... | collective-permute-start | bytes 1179656 | tf_op jit(solution)/shard_map/ppermute | solution.py:219
  7.3 0.0 collective-permute-start.2
  7.3 0.0 collective-permute-start.1
  7.3 0.0 collective-permute-start
  7.3 3.3 %collective-permute-start.9 = (bf16[256,768]{1,0:T(8,128)(2,1)}, bf16[256,768]{1,0:T(8,128)(2,1)S(1)}, u32[]{:S(2)}, u32[]{:S(2)}) collective-permute-start(bf16[256,768]{1,0:T(8,128)(2,1)} %bitcast.18), channel_id=1, source_target_pairs={{0,8},{1,9},{2,10},{3,11},{4,12},{5,13},{6,14},{7,15},{8,0},{9,1},... | collective-permute-start | bytes 1179656 | tf_op jit(solution)/shard_map/ppermute | solution.py:219
  10.6 2.0 %collective-permute-done.5.g0 = bf16[256,768]{1,0:T(8,128)(2,1)S(1)} collective-permute-done((bf16[256,768]{1,0:T(8,128)(2,1)S(1)}, bf16[256,768]{1,0:T(8,128)(2,1)S(1)}, u32[]{:S(2)}, u32[]{:S(2)}) %collective-permute-start.5) | collective-permute-done | bytes 393248 | tf_op jit(solution)/shard_map/ppermute | solution.py:219
  12.6 0.5 collective-permute-start.8
  13.1 6.7 %collective-permute-done.2.x2 = bf16[256,768]{1,0:T(8,128)(2,1)S(1)} collective-permute-done((bf16[256,768]{1,0:T(8,128)(2,1)S(1)}, bf16[256,768]{1,0:T(8,128)(2,1)S(1)}, u32[]{:S(2)}, u32[]{:S(2)}) %collective-permute-start.2) | collective-permute-done | bytes 393248 | tf_op jit(solution)/shard_map/ppermute | solution.py:219
  19.8 3.2 %collective-permute-start.7 = (bf16[256,768]{1,0:T(8,128)(2,1)S(1)}, bf16[256,768]{1,0:T(8,128)(2,1)S(1)}, u32[]{:S(2)}, u32[]{:S(2)}) collective-permute-start(bf16[256,768]{1,0:T(8,128)(2,1)S(1)} %collective-permute-done.5.g0), channel_id=1, source_target_pairs={{0,8},{1,9},{2,10},{3,11},{4,12},{5,13},{6,14},{7,15},{8,0},{9,1},... | collective-permute-start | bytes 1179656 | tf_op jit(solution)/shard_map/ppermute | solution.py:219
  23.0 0.0 collective-permute-done.1.x1
  23.0 1.1 %collective-permute-start.6 = (bf16[256,768]{1,0:T(8,128)(2,1)S(1)}, bf16[256,768]{1,0:T(8,128)(2,1)S(1)}, u32[]{:S(2)}, u32[]{:S(2)}) collective-permute-start(bf16[256,768]{1,0:T(8,128)(2,1)S(1)} %collective-permute-done.5.g0), channel_id=1, source_target_pairs={{0,1},{1,0},{2,3},{3,2},{4,5},{5,4},{6,7},{7,6},{8,9},{9,8},{10,11... | collective-permute-start | bytes 1179656 | tf_op jit(solution)/shard_map/ppermute | solution.py:219
  24.1 2.4 %stage.1 = (bf16[6,3,256,256]{3,2,1,0:T(8,128)(2,1)S(1)}, bf16[6,3,256,256]{3,2,1,0:T(8,128)(2,1)S(1)}) custom-call(bf16[6,3,256,256]{3,2,1,0:T(8,128)(2,1)} %bitcast.13, bf16[6,3,256,256]{3,2,1,0:T(8,128)(2,1)} %bitcast.14), custom_call_target="tpu_custom_call" | custom-call | bytes 9437184 | tf_op jit(solution)/shard_map/stage/pallas_call | solution.py:174
  26.5 0.3 collective-permute-done.x0
  26.8 2.5 %shard_map.120 = (f32[256,768]{1,0:T(8,128)S(1)}, bf16[256,768]{1,0:T(8,128)(2,1)S(1)}, bf16[256,768]{1,0:T(8,128)(2,1)S(1)}) custom-call(s32[3,6]{1,0:T(4,128)S(1)} %get-tuple-element.22.cin, s32[3,6]{1,0:T(4,128)S(1)} %get-tuple-element.23.cout, bf16[256,768]{1,0:T(8,128)(2,1)S(1)} %collective-permute-done.x0, ...), custom_call_target="tpu_custom_call" | custom-call | flops 1207959552 | bytes 7471104 | tf_op jit(solution)/shard_map/pallas_call | solution.py:192
  29.3 0.7 %collective-permute-start.3 = (bf16[256,768]{1,0:T(8,128)(2,1)S(1)}, bf16[256,768]{1,0:T(8,128)(2,1)S(1)}, u32[]{:S(2)}, u32[]{:S(2)}) collective-permute-start(bf16[256,768]{1,0:T(8,128)(2,1)S(1)} %get-tuple-element.28), channel_id=1, source_target_pairs={{0,1},{1,0},{2,3},{3,2},{4,5},{5,4},{6,7},{7,6},{8,9},{9,8},{10,11... | collective-permute-start | bytes 1179656 | tf_op jit(solution)/shard_map/ppermute | solution.py:219
  30.1 0.3 collective-permute-done.9.x2
  30.4 0.0 collective-permute-start.4
  30.4 0.0 collective-permute-done.8.x1
  30.4 2.0 %shard_map.121 = (bf16[256,1536]{1,0:T(8,128)(2,1)S(1)}, f32[256,1536]{1,0:T(8,128)S(1)}) custom-call(s32[3,6]{1,0:T(4,128)S(1)} %get-tuple-element.22.cin, bf16[256,768]{1,0:T(8,128)(2,1)S(1)} %get-tuple-element.31.x0, bf16[256,768]{1,0:T(8,128)(2,1)S(1)} %collective-permute-done.8.x1, bf16[256,768]{1,0:T(8,128)(2,1)S(1)} %collective-permute-done.9.x2, ...), custom_call_target="tpu_custom_call" | custom-call | flops 603979776 | bytes 5898240 | tf_op jit(solution)/shard_map/pallas_call | solution.py:192
  32.4 6.4 %collective-permute-done.7.g2 = bf16[256,768]{1,0:T(8,128)(2,1)S(1)} collective-permute-done((bf16[256,768]{1,0:T(8,128)(2,1)S(1)}, bf16[256,768]{1,0:T(8,128)(2,1)S(1)}, u32[]{:S(2)}, u32[]{:S(2)}) %collective-permute-start.7) | collective-permute-done | bytes 393248 | tf_op jit(solution)/shard_map/ppermute | solution.py:219
  38.8 0.0 collective-permute-done.6.g1
  38.8 2.6 %shard_map.122 = (f32[256,768]{1,0:T(8,128)S(1)}, bf16[256,768]{1,0:T(8,128)(2,1)S(1)}, bf16[256,768]{1,0:T(8,128)(2,1)S(1)}, bf16[256,1536]{1,0:T(8,128)(2,1)S(1)}) custom-call(s32[3,6]{1,0:T(4,128)S(1)} %get-tuple-element.22.cin, s32[3,6]{1,0:T(4,128)S(1)} %get-tuple-element.23.cout, bf16[256,768]{1,0:T(8,128)(2,1)S(1)} %collective-permute-done.5.g0, ...), custom_call_target="tpu_custom_call" | custom-call | flops 1207959552 | bytes 9830400 | tf_op jit(solution)/shard_map/pallas_call | solution.py:192
  41.4 1.1 %collective-permute-start.10 = (bf16[256,768]{1,0:T(8,128)(2,1)S(1)}, bf16[256,768]{1,0:T(8,128)(2,1)S(1)}, u32[]{:S(2)}, u32[]{:S(2)}) collective-permute-start(bf16[256,768]{1,0:T(8,128)(2,1)S(1)} %get-tuple-element.34), channel_id=1, source_target_pairs={{0,1},{1,0},{2,3},{3,2},{4,5},{5,4},{6,7},{7,6},{8,9},{9,8},{10,11... | collective-permute-start | bytes 1179656 | tf_op jit(solution)/shard_map/ppermute | solution.py:219
  42.4 1.0 %collective-permute-start.11 = (bf16[256,768]{1,0:T(8,128)(2,1)S(1)}, bf16[256,768]{1,0:T(8,128)(2,1)S(1)}, u32[]{:S(2)}, u32[]{:S(2)}) collective-permute-start(bf16[256,768]{1,0:T(8,128)(2,1)S(1)} %get-tuple-element.35), channel_id=1, source_target_pairs={{0,8},{1,9},{2,10},{3,11},{4,12},{5,13},{6,14},{7,15},{8,0},{9,1},... | collective-permute-start | bytes 1179656 | tf_op jit(solution)/shard_map/ppermute | solution.py:219
  43.5 3.3 %shard_map.123 = (bf16[6,3,256,256]{3,2,1,0:T(8,128)(2,1)}, bf16[6,3,256,256]{3,2,1,0:T(8,128)(2,1)}) custom-call(s32[3,6]{1,0:T(4,128)S(1)} %get-tuple-element.22.cin, s32[3,6]{1,0:T(4,128)S(1)} %get-tuple-element.23.cout, bf16[256,768]{1,0:T(8,128)(2,1)S(1)} %get-tuple-element.31.x0, bf16[256,768]{1,0:T(8,128)(2,1)S(1)} %collective-permute-done.8.x1, ...), custom_call_target="tpu_custom_call" | custom-call | flops 1207959552 | bytes 8650752 | tf_op jit(solution)/shard_map/pallas_call | solution.py:192
  46.8 0.0 collective-permute-done.3
  46.8 0.4 collective-permute-done.4
  47.2 0.9 %fusion = bf16[1,256,768]{2,1,0:T(8,128)(2,1)} fusion(bf16[256,768]{1,0:T(8,128)(2,1)S(1)} %collective-permute-done.4, f32[256,768]{1,0:T(8,128)S(1)} %get-tuple-element.27, bf16[256,768]{1,0:T(8,128)(2,1)S(1)} %collective-permute-done.3), kind=kLoop, calls=%fused_computation.2 | loop fusion | flops 983040 | bytes 1966080 | tf_op jit(solution)/shard_map/broadcast_in_dim | solution.py:266
  48.1 3.9 %collective-permute-done.10 = bf16[256,768]{1,0:T(8,128)(2,1)S(1)} collective-permute-done((bf16[256,768]{1,0:T(8,128)(2,1)S(1)}, bf16[256,768]{1,0:T(8,128)(2,1)S(1)}, u32[]{:S(2)}, u32[]{:S(2)}) %collective-permute-start.10) | collective-permute-done | bytes 393248 | tf_op jit(solution)/shard_map/ppermute | solution.py:219
  52.0 2.1 %collective-permute-done.11 = bf16[256,768]{1,0:T(8,128)(2,1)S(1)} collective-permute-done((bf16[256,768]{1,0:T(8,128)(2,1)S(1)}, bf16[256,768]{1,0:T(8,128)(2,1)S(1)}, u32[]{:S(2)}, u32[]{:S(2)}) %collective-permute-start.11) | collective-permute-done | bytes 393248 | tf_op jit(solution)/shard_map/ppermute | solution.py:219
  54.1 0.9 %fusion.1 = bf16[1,256,768]{2,1,0:T(8,128)(2,1)} fusion(bf16[256,768]{1,0:T(8,128)(2,1)S(1)} %collective-permute-done.11, f32[256,768]{1,0:T(8,128)S(1)} %get-tuple-element.33, bf16[256,768]{1,0:T(8,128)(2,1)S(1)} %collective-permute-done.10), kind=kLoop, calls=%fused_computation.3 | loop fusion | flops 983040 | bytes 1966080 | tf_op jit(solution)/shard_map/broadcast_in_dim | solution.py:266
Async XLA Ops:
  2.0 10.6 %collective-permute-start.5 = (bf16[256,768]{1,0:T(8,128)(2,1)S(1)}, bf16[256,768]{1,0:T(8,128)(2,1)S(1)}, u32[]{:S(2)}, u32[]{:S(2)}) collective-permute-start(bf16[256,768]{1,0:T(8,128)(2,1)S(1)} %get-tuple-element.30), channel_id=1, source_target_pairs={{0,240},{1,241},{2,242},{3,243},{4,244},{5,245},{6,246},{7,247},{8... | collective-permute-start | bytes 1179656 | tf_op jit(solution)/shard_map/ppermute | solution.py:219
  7.3 12.5 %collective-permute-start.2 = (bf16[256,768]{1,0:T(8,128)(2,1)S(1)}, bf16[256,768]{1,0:T(8,128)(2,1)S(1)}, u32[]{:S(2)}, u32[]{:S(2)}) collective-permute-start(bf16[256,768]{1,0:T(8,128)(2,1)S(1)} %get-tuple-element.24), channel_id=1, source_target_pairs={{0,24},{1,25},{2,26},{3,27},{4,28},{5,29},{6,30},{7,31},{8,16},{9,... | collective-permute-start | bytes 1179656 | tf_op jit(solution)/shard_map/ppermute | solution.py:219
  7.3 15.7 %collective-permute-start.1 = (bf16[256,768]{1,0:T(8,128)(2,1)S(1)}, bf16[256,768]{1,0:T(8,128)(2,1)S(1)}, u32[]{:S(2)}, u32[]{:S(2)}) collective-permute-start(bf16[256,768]{1,0:T(8,128)(2,1)S(1)} %get-tuple-element.24), channel_id=1, source_target_pairs={{0,17},{1,16},{2,19},{3,18},{4,21},{5,20},{6,23},{7,22},{8,25},{9,... | collective-permute-start | bytes 1179656 | tf_op jit(solution)/shard_map/ppermute | solution.py:219
  7.3 19.5 %collective-permute-start = (bf16[256,768]{1,0:T(8,128)(2,1)S(1)}, bf16[256,768]{1,0:T(8,128)(2,1)S(1)}, u32[]{:S(2)}, u32[]{:S(2)}) collective-permute-start(bf16[256,768]{1,0:T(8,128)(2,1)S(1)} %get-tuple-element.24), channel_id=1, source_target_pairs={{0,16},{1,17},{2,18},{3,19},{4,20},{5,21},{6,22},{7,23},{8,24},{9,... | collective-permute-start | bytes 1179656 | tf_op jit(solution)/shard_map/ppermute | solution.py:219
  7.3 23.1 %collective-permute-start.9 = (bf16[256,768]{1,0:T(8,128)(2,1)}, bf16[256,768]{1,0:T(8,128)(2,1)S(1)}, u32[]{:S(2)}, u32[]{:S(2)}) collective-permute-start(bf16[256,768]{1,0:T(8,128)(2,1)} %bitcast.18), channel_id=1, source_target_pairs={{0,8},{1,9},{2,10},{3,11},{4,12},{5,13},{6,14},{7,15},{8,0},{9,1},... | collective-permute-start | bytes 1179656 | tf_op jit(solution)/shard_map/ppermute | solution.py:219
  12.6 17.8 %collective-permute-start.8 = (bf16[256,768]{1,0:T(8,128)(2,1)}, bf16[256,768]{1,0:T(8,128)(2,1)S(1)}, u32[]{:S(2)}, u32[]{:S(2)}) collective-permute-start(bf16[256,768]{1,0:T(8,128)(2,1)} %bitcast.19), channel_id=1, source_target_pairs={{0,1},{1,0},{2,3},{3,2},{4,5},{5,4},{6,7},{7,6},{8,9},{9,8},{10,11... | collective-permute-start | bytes 1179656 | tf_op jit(solution)/shard_map/ppermute | solution.py:219
  19.8 19.0 %collective-permute-start.7 = (bf16[256,768]{1,0:T(8,128)(2,1)S(1)}, bf16[256,768]{1,0:T(8,128)(2,1)S(1)}, u32[]{:S(2)}, u32[]{:S(2)}) collective-permute-start(bf16[256,768]{1,0:T(8,128)(2,1)S(1)} %collective-permute-done.5.g0), channel_id=1, source_target_pairs={{0,8},{1,9},{2,10},{3,11},{4,12},{5,13},{6,14},{7,15},{8,0},{9,1},... | collective-permute-start | bytes 1179656 | tf_op jit(solution)/shard_map/ppermute | solution.py:219
  23.0 15.8 %collective-permute-start.6 = (bf16[256,768]{1,0:T(8,128)(2,1)S(1)}, bf16[256,768]{1,0:T(8,128)(2,1)S(1)}, u32[]{:S(2)}, u32[]{:S(2)}) collective-permute-start(bf16[256,768]{1,0:T(8,128)(2,1)S(1)} %collective-permute-done.5.g0), channel_id=1, source_target_pairs={{0,1},{1,0},{2,3},{3,2},{4,5},{5,4},{6,7},{7,6},{8,9},{9,8},{10,11... | collective-permute-start | bytes 1179656 | tf_op jit(solution)/shard_map/ppermute | solution.py:219
  29.3 17.4 %collective-permute-start.3 = (bf16[256,768]{1,0:T(8,128)(2,1)S(1)}, bf16[256,768]{1,0:T(8,128)(2,1)S(1)}, u32[]{:S(2)}, u32[]{:S(2)}) collective-permute-start(bf16[256,768]{1,0:T(8,128)(2,1)S(1)} %get-tuple-element.28), channel_id=1, source_target_pairs={{0,1},{1,0},{2,3},{3,2},{4,5},{5,4},{6,7},{7,6},{8,9},{9,8},{10,11... | collective-permute-start | bytes 1179656 | tf_op jit(solution)/shard_map/ppermute | solution.py:219
  30.4 16.9 %collective-permute-start.4 = (bf16[256,768]{1,0:T(8,128)(2,1)S(1)}, bf16[256,768]{1,0:T(8,128)(2,1)S(1)}, u32[]{:S(2)}, u32[]{:S(2)}) collective-permute-start(bf16[256,768]{1,0:T(8,128)(2,1)S(1)} %get-tuple-element.29), channel_id=1, source_target_pairs={{0,8},{1,9},{2,10},{3,11},{4,12},{5,13},{6,14},{7,15},{8,0},{9,1},... | collective-permute-start | bytes 1179656 | tf_op jit(solution)/shard_map/ppermute | solution.py:219
  41.4 10.7 %collective-permute-start.10 = (bf16[256,768]{1,0:T(8,128)(2,1)S(1)}, bf16[256,768]{1,0:T(8,128)(2,1)S(1)}, u32[]{:S(2)}, u32[]{:S(2)}) collective-permute-start(bf16[256,768]{1,0:T(8,128)(2,1)S(1)} %get-tuple-element.34), channel_id=1, source_target_pairs={{0,1},{1,0},{2,3},{3,2},{4,5},{5,4},{6,7},{7,6},{8,9},{9,8},{10,11... | collective-permute-start | bytes 1179656 | tf_op jit(solution)/shard_map/ppermute | solution.py:219
  42.4 11.7 %collective-permute-start.11 = (bf16[256,768]{1,0:T(8,128)(2,1)S(1)}, bf16[256,768]{1,0:T(8,128)(2,1)S(1)}, u32[]{:S(2)}, u32[]{:S(2)}) collective-permute-start(bf16[256,768]{1,0:T(8,128)(2,1)S(1)} %get-tuple-element.35), channel_id=1, source_target_pairs={{0,8},{1,9},{2,10},{3,11},{4,12},{5,13},{6,14},{7,15},{8,0},{9,1},... | collective-permute-start | bytes 1179656 | tf_op jit(solution)/shard_map/ppermute | solution.py:219
where the time goes:
time: 55.1 us; the launch traced here: 55 us
  waiting for transfers between devices  22.1 us (40%)
  starting transfers between devices  16.3 us (30%)
  Pallas kernels  14.1 us (26%)
  other arithmetic  1.76 us (3%)
  between operations  0.7 us (1%)
    ppermute x12, waiting for transfers between devices, send(): return lax.ppermute(value, ('pipe', 'tensor'), route)  22.1 us
    ppermute x12, starting transfers between devices, send(): return lax.ppermute(value, ('pipe', 'tensor'), route)  16.3 us
    pallas_call x4, Pallas kernels, run(): pl.pallas_call(body, in_specs=[SMEM] * len(tables) + [VMEM] * len(ins), o...  10.4 us
    pallas_call x1, Pallas kernels, stage(): pl.pallas_call(stage_kernel, in_specs=[HBM] * 2, out_specs=(VMEM,) * 2, s...  2.4 us
    broadcast_in_dim x2, other arithmetic, shards(): return (out_acts[None], in_grads[None], gw_in[None], gw_out[None])  1.76 us
    pallas_call x1, Pallas kernels, pick(): pl.pallas_call(functools.partial(pick_kernel, lax.axis_size('pipe')), in_...  1.32 us
  transfers between devices with their start and end apart: 12, of which 8 were waited for; matrix products, arithmetic and copies ran while one was open for 2% of the time, Pallas kernels for 23%

commit v1 on v0

--- a/solution.py
+++ b/solution.py
@@ -70,7 +70,9 @@
         slope[:, h * size : (h + 1) * size] = rate
 
 
-def backward_kernel(cin, cout, g0, g1, g2, slope, w_in, w_out, own, c1, c2, dpre, acc):
+def backward_kernel(
+    cin, cout, g0, g1, g2, slope, w_in, w_out, own, c1_top, c2_top, c1_low, c2_low, dpre, acc
+):
     hidden, slots, size, _ = w_in.shape
     own[...] = g0[...].astype(F32)
     acc[...] = jnp.zeros_like(acc)
@@ -84,8 +86,11 @@
         dpre[:, h * size : (h + 1) * size] = grad
         for k in range(slots):
             sums[k][:, column(cin, h, k, size)] += dot(grad, w_in[h, k], NT)
-    c1[...] = acc[0].astype(BF)
-    c2[...] = acc[1].astype(BF)
+    top = c1_top.shape[0]
+    c1_top[...] = acc[0, :top].astype(BF)
+    c2_top[...] = acc[1, :top].astype(BF)
+    c1_low[...] = acc[0, top:].astype(BF)
+    c2_low[...] = acc[1, top:].astype(BF)
 
 
 def weights_kernel(
@@ -185,6 +190,31 @@
     )(*in_hbm(w_in, w_out))
 
 
+def finish_kernel(first, own, c1, c2, *rest):
+    out, buf, sem = rest[-3:]
+    rows = pl.ds(first, c1.shape[0])
+    buf[...] = (own[rows, :] + c1[...].astype(F32) + c2[...].astype(F32)).astype(BF)
+    copy = pltpu.make_async_copy(buf, out.at[rows, :], sem)
+    copy.start()
+    copy.wait()
+
+
+def finish(first, own, c1, c2, begun=()):
+    return pl.pallas_call(
+        functools.partial(finish_kernel, first),
+        in_specs=[VMEM] * 3 + [HBM] * len(begun),
+        out_specs=HBM,
+        scratch_shapes=[pltpu.VMEM(c1.shape, BF), pltpu.SemaphoreType.DMA],
+        out_shape=jax.ShapeDtypeStruct(own.shape, BF),
+        input_output_aliases={3: 0} if begun else {},
+        cost_estimate=pl.CostEstimate(
+            flops=2 * c1.size, bytes_accessed=10 * c1.size, transcendentals=0
+        ),
+        compiler_params=pltpu.CompilerParams(vmem_limit_bytes=4 << 20),
+        name="finish",
+    )(own, c1, c2, *begun)
+
+
 def run(body, tables, ins, outs, out_spec, scratch, flops):
     size = sum(x.size * x.dtype.itemsize for x in ins) + sum(
         x.size * jnp.dtype(x.dtype).itemsize for x in outs
@@ -251,18 +281,23 @@
         2 * unit,
     )
     a1, a2 = exchange((a1, a2))
-    own_b, b1, b2, dpre = run(
-        backward_kernel, (cin, cout), (*gb, slope_b, w_in, w_out), (total, act, act, hid_bf),
-        VMEM, [acc], 2 * unit,
+    cut = tokens - tokens // 4
+    top = jax.ShapeDtypeStruct((cut, width), BF)
+    low = jax.ShapeDtypeStruct((tokens - cut, width), BF)
+    own_b, b1, b2, b1_low, b2_low, dpre = run(
+        backward_kernel, (cin, cout), (*gb, slope_b, w_in, w_out),
+        (total, top, top, low, low, hid_bf), VMEM, [acc], 2 * unit,
     )
     b1, b2 = exchange((b1, b2))
+    b1_low, b2_low = exchange((b1_low, b2_low))
     held = pltpu.VMEM(w_in.shape, BF)
     gw_in, gw_out = run(
         weights_kernel, (cin, cout), (*xb, *gb, hid_b, dpre), (weight, weight), HBM,
         [held, held, pltpu.SemaphoreType.DMA((2, hidden))], 2 * unit,
     )
     out_acts = (own_a + a1.astype(F32) + a2.astype(F32)).astype(BF)
-    in_grads = (own_b + b1.astype(F32) + b2.astype(F32)).astype(BF)
+    in_grads = finish(0, own_b, b1, b2)
+    in_grads = finish(cut, own_b, b1_low, b2_low, (in_grads,))
     return (out_acts[None], in_grads[None], gw_in[None], gw_out[None])
 
 

time: 55.1 us -> 57.4 us (1.042)
  the two profiles are of different devices: /device:TPU:2 before, /device:TPU:102 now
where the time goes in v1:
time: 57.4 us; the launch traced here: 57.3 us
  waiting for transfers between devices  25 us (44%)
  Pallas kernels  15.5 us (27%)
  starting transfers between devices  15.1 us (26%)
  other arithmetic  0.89 us (2%)
  between operations  0.74 us (1%)
    ppermute x14, waiting for transfers between devices, send(): return lax.ppermute(value, ('pipe', 'tensor'), route)  25 us
    ppermute x14, starting transfers between devices, send(): return lax.ppermute(value, ('pipe', 'tensor'), route)  15.1 us
    pallas_call x4, Pallas kernels, run(): pl.pallas_call(body, in_specs=[SMEM] * len(tables) + [VMEM] * len(ins), o...  10.3 us
    pallas_call x1, Pallas kernels, stage(): pl.pallas_call(stage_kernel, in_specs=[HBM] * 2, out_specs=(VMEM,) * 2, s...  2.4 us
    pallas_call x2, Pallas kernels, finish(): pl.pallas_call(functools.partial(finish_kernel, first), in_specs=[VMEM] *...  1.51 us
    pallas_call x1, Pallas kernels, pick(): pl.pallas_call(functools.partial(pick_kernel, lax.axis_size('pipe')), in_...  1.32 us
  transfers between devices with their start and end apart: 14, of which 7 were waited for; matrix products, arithmetic and copies ran while one was open for 2% of the time, Pallas kernels for 24%

profile of v1, /device:TPU:102, one launch (start us, length us, event | category | flops | bytes accessed | tf_op | source)
XLA Modules:
  0.0 57.3 jit_solution(6221189197545426893)
XLA Ops:
  0.6 1.3 %pick.1 = (bf16[256,768]{1,0:T(8,128)(2,1)S(1)}, bf16[256,768]{1,0:T(8,128)(2,1)S(1)}, bf16[256,768]{1,0:T(8,128)(2,1)S(1)}, s32[3,6]{1,0:T(4,128)S(1)}, s32[3,6]{1,0:T(4,128)S(1)}) custom-call(bf16[256,768]{1,0:T(8,128)(2,1)} %bitcast.15, bf16[256,768]{1,0:T(8,128)(2,1)} %first_a.1, bf16[256,768]{1,0:T(8,128)(2,1)} %bitcast.16, bf16[256,768]{1,0:T(8,128)(2,1)} %last_g.1, ...), custom_call_target="tpu_custom_call" | custom-call | bytes 2359296 | tf_op jit(solution)/shard_map/pick/pallas_call | solution.py:151
  2.0 0.0 collective-permute-start.5
  2.0 3.3 %collective-permute-start.2 = (bf16[256,768]{1,0:T(8,128)(2,1)S(1)}, bf16[256,768]{1,0:T(8,128)(2,1)S(1)}, u32[]{:S(2)}, u32[]{:S(2)}) collective-permute-start(bf16[256,768]{1,0:T(8,128)(2,1)S(1)} %get-tuple-element.26), channel_id=1, source_target_pairs={{0,24},{1,25},{2,26},{3,27},{4,28},{5,29},{6,30},{7,31},{8,16},{9,... | collective-permute-start | bytes 1179656 | tf_op jit(solution)/shard_map/ppermute | solution.py:249
  5.3 3.1 %collective-permute-start.1 = (bf16[256,768]{1,0:T(8,128)(2,1)S(1)}, bf16[256,768]{1,0:T(8,128)(2,1)S(1)}, u32[]{:S(2)}, u32[]{:S(2)}) collective-permute-start(bf16[256,768]{1,0:T(8,128)(2,1)S(1)} %get-tuple-element.26), channel_id=1, source_target_pairs={{0,17},{1,16},{2,19},{3,18},{4,21},{5,20},{6,23},{7,22},{8,25},{9,... | collective-permute-start | bytes 1179656 | tf_op jit(solution)/shard_map/ppermute | solution.py:249
  8.4 0.4 collective-permute-start
  8.8 0.3 collective-permute-start.9
  9.1 0.0 collective-permute-done.5.g0
  9.1 1.2 %collective-permute-start.8 = (bf16[256,768]{1,0:T(8,128)(2,1)}, bf16[256,768]{1,0:T(8,128)(2,1)S(1)}, u32[]{:S(2)}, u32[]{:S(2)}) collective-permute-start(bf16[256,768]{1,0:T(8,128)(2,1)} %bitcast.19), channel_id=1, source_target_pairs={{0,1},{1,0},{2,3},{3,2},{4,5},{5,4},{6,7},{7,6},{8,9},{9,8},{10,11... | collective-permute-start | bytes 1179656 | tf_op jit(solution)/shard_map/ppermute | solution.py:249
  10.3 8.3 %collective-permute-done.2.x2 = bf16[256,768]{1,0:T(8,128)(2,1)S(1)} collective-permute-done((bf16[256,768]{1,0:T(8,128)(2,1)S(1)}, bf16[256,768]{1,0:T(8,128)(2,1)S(1)}, u32[]{:S(2)}, u32[]{:S(2)}) %collective-permute-start.2) | collective-permute-done | bytes 393248 | tf_op jit(solution)/shard_map/ppermute | solution.py:249
  18.6 1.9 %collective-permute-done.1.x1 = bf16[256,768]{1,0:T(8,128)(2,1)S(1)} collective-permute-done((bf16[256,768]{1,0:T(8,128)(2,1)S(1)}, bf16[256,768]{1,0:T(8,128)(2,1)S(1)}, u32[]{:S(2)}, u32[]{:S(2)}) %collective-permute-start.1) | collective-permute-done | bytes 393248 | tf_op jit(solution)/shard_map/ppermute | solution.py:249
  20.5 1.6 %collective-permute-start.6 = (bf16[256,768]{1,0:T(8,128)(2,1)S(1)}, bf16[256,768]{1,0:T(8,128)(2,1)S(1)}, u32[]{:S(2)}, u32[]{:S(2)}) collective-permute-start(bf16[256,768]{1,0:T(8,128)(2,1)S(1)} %collective-permute-done.5.g0), channel_id=1, source_target_pairs={{0,1},{1,0},{2,3},{3,2},{4,5},{5,4},{6,7},{7,6},{8,9},{9,8},{10,11... | collective-permute-start | bytes 1179656 | tf_op jit(solution)/shard_map/ppermute | solution.py:249
  22.1 2.4 %stage.1 = (bf16[6,3,256,256]{3,2,1,0:T(8,128)(2,1)S(1)}, bf16[6,3,256,256]{3,2,1,0:T(8,128)(2,1)S(1)}) custom-call(bf16[6,3,256,256]{3,2,1,0:T(8,128)(2,1)} %bitcast.12, bf16[6,3,256,256]{3,2,1,0:T(8,128)(2,1)} %bitcast.13), custom_call_target="tpu_custom_call" | custom-call | bytes 9437184 | tf_op jit(solution)/shard_map/stage/pallas_call | solution.py:179
  24.5 0.0 collective-permute-done.x0
  24.5 2.5 %shard_map.120 = (f32[256,768]{1,0:T(8,128)S(1)}, bf16[256,768]{1,0:T(8,128)(2,1)S(1)}, bf16[256,768]{1,0:T(8,128)(2,1)S(1)}) custom-call(s32[3,6]{1,0:T(4,128)S(1)} %get-tuple-element.24.cin, s32[3,6]{1,0:T(4,128)S(1)} %get-tuple-element.25.cout, bf16[256,768]{1,0:T(8,128)(2,1)S(1)} %collective-permute-done.x0, ...), custom_call_target="tpu_custom_call" | custom-call | flops 1207959552 | bytes 7471104 | tf_op jit(solution)/shard_map/pallas_call | solution.py:222
  27.0 0.6 collective-permute-start.3
  27.6 1.6 %collective-permute-start.4 = (bf16[256,768]{1,0:T(8,128)(2,1)S(1)}, bf16[256,768]{1,0:T(8,128)(2,1)S(1)}, u32[]{:S(2)}, u32[]{:S(2)}) collective-permute-start(bf16[256,768]{1,0:T(8,128)(2,1)S(1)} %get-tuple-element.31), channel_id=1, source_target_pairs={{0,8},{1,9},{2,10},{3,11},{4,12},{5,13},{6,14},{7,15},{8,0},{9,1},... | collective-permute-start | bytes 1179656 | tf_op jit(solution)/shard_map/ppermute | solution.py:249
  29.2 1.5 %collective-permute-done.8.x1 = bf16[256,768]{1,0:T(8,128)(2,1)S(1)} collective-permute-done((bf16[256,768]{1,0:T(8,128)(2,1)}, bf16[256,768]{1,0:T(8,128)(2,1)S(1)}, u32[]{:S(2)}, u32[]{:S(2)}) %collective-permute-start.8) | collective-permute-done | bytes 393248 | tf_op jit(solution)/shard_map/ppermute | solution.py:249
  30.7 2.0 %shard_map.121 = (bf16[256,1536]{1,0:T(8,128)(2,1)S(1)}, f32[256,1536]{1,0:T(8,128)S(1)}) custom-call(s32[3,6]{1,0:T(4,128)S(1)} %get-tuple-element.24.cin, bf16[256,768]{1,0:T(8,128)(2,1)S(1)} %get-tuple-element.33.x0, bf16[256,768]{1,0:T(8,128)(2,1)S(1)} %collective-permute-done.8.x1, bf16[256,768]{1,0:T(8,128)(2,1)S(1)} %collective-permute-done.9.x2, ...), custom_call_target="tpu_custom_call" | custom-call | flops 603979776 | bytes 5898240 | tf_op jit(solution)/shard_map/pallas_call | solution.py:222
  32.7 6.4 %collective-permute-done.6.g1 = bf16[256,768]{1,0:T(8,128)(2,1)S(1)} collective-permute-done((bf16[256,768]{1,0:T(8,128)(2,1)S(1)}, bf16[256,768]{1,0:T(8,128)(2,1)S(1)}, u32[]{:S(2)}, u32[]{:S(2)}) %collective-permute-start.6) | collective-permute-done | bytes 393248 | tf_op jit(solution)/shard_map/ppermute | solution.py:249
  39.1 2.5 %shard_map.122 = (f32[256,768]{1,0:T(8,128)S(1)}, bf16[192,768]{1,0:T(8,128)(2,1)S(1)}, bf16[192,768]{1,0:T(8,128)(2,1)S(1)}, bf16[64,768]{1,0:T(8,128)(2,1)S(1)...) custom-call(s32[3,6]{1,0:T(4,128)S(1)} %get-tuple-element.24.cin, s32[3,6]{1,0:T(4,128)S(1)} %get-tuple-element.25.cout, ...), custom_call_target="tpu_custom_call" | custom-call | flops 1207959552 | bytes 9830400 | tf_op jit(solution)/shard_map/pallas_call | solution.py:222
  41.6 0.9 %collective-permute-start.10 = (bf16[64,768]{1,0:T(8,128)(2,1)S(1)}, bf16[64,768]{1,0:T(8,128)(2,1)S(1)}, u32[]{:S(2)}, u32[]{:S(2)}) collective-permute-start(bf16[64,768]{1,0:T(8,128)(2,1)S(1)} %get-tuple-element.36), channel_id=1, source_target_pairs={{0,1},{1,0},{2,3},{3,2},{4,5},{5,4},{6,7},{7,6},{8,9},{9,8},{10,11... | collective-permute-start | bytes 294920 | tf_op jit(solution)/shard_map/ppermute | solution.py:249
  42.5 0.3 collective-permute-start.11
  42.8 1.3 %collective-permute-start.12 = (bf16[192,768]{1,0:T(8,128)(2,1)S(1)}, bf16[192,768]{1,0:T(8,128)(2,1)S(1)}, u32[]{:S(2)}, u32[]{:S(2)}) collective-permute-start(bf16[192,768]{1,0:T(8,128)(2,1)S(1)} %get-tuple-element.38), channel_id=1, source_target_pairs={{0,1},{1,0},{2,3},{3,2},{4,5},{5,4},{6,7},{7,6},{8,9},{9,8},{10,11... | collective-permute-start | bytes 884744 | tf_op jit(solution)/shard_map/ppermute | solution.py:249
  44.1 3.4 %collective-permute-done.3 = bf16[256,768]{1,0:T(8,128)(2,1)S(1)} collective-permute-done((bf16[256,768]{1,0:T(8,128)(2,1)S(1)}, bf16[256,768]{1,0:T(8,128)(2,1)S(1)}, u32[]{:S(2)}, u32[]{:S(2)}) %collective-permute-start.3) | collective-permute-done | bytes 393248 | tf_op jit(solution)/shard_map/ppermute | solution.py:249
  47.5 0.5 collective-permute-start.13
  48.0 0.0 collective-permute-done.4
  48.0 0.9 %fusion = bf16[1,256,768]{2,1,0:T(8,128)(2,1)} fusion(bf16[256,768]{1,0:T(8,128)(2,1)S(1)} %collective-permute-done.4, f32[256,768]{1,0:T(8,128)S(1)} %get-tuple-element.29, bf16[256,768]{1,0:T(8,128)(2,1)S(1)} %collective-permute-done.3), kind=kLoop, calls=%fused_computation.1 | loop fusion | flops 983040 | bytes 1966080 | tf_op jit(solution)/shard_map/broadcast_in_dim | solution.py:301
  48.9 3.3 %shard_map.123 = (bf16[6,3,256,256]{3,2,1,0:T(8,128)(2,1)}, bf16[6,3,256,256]{3,2,1,0:T(8,128)(2,1)}) custom-call(s32[3,6]{1,0:T(4,128)S(1)} %get-tuple-element.24.cin, s32[3,6]{1,0:T(4,128)S(1)} %get-tuple-element.25.cout, bf16[256,768]{1,0:T(8,128)(2,1)S(1)} %get-tuple-element.33.x0, bf16[256,768]{1,0:T(8,128)(2,1)S(1)} %collective-permute-done.8.x1, ...), custom_call_target="tpu_custom_call" | custom-call | flops 1207959552 | bytes 8650752 | tf_op jit(solution)/shard_map/pallas_call | solution.py:222
  52.2 1.1 %collective-permute-done.12.c1 = bf16[192,768]{1,0:T(8,128)(2,1)S(1)} collective-permute-done((bf16[192,768]{1,0:T(8,128)(2,1)S(1)}, bf16[192,768]{1,0:T(8,128)(2,1)S(1)}, u32[]{:S(2)}, u32[]{:S(2)}) %collective-permute-start.12) | collective-permute-done | bytes 294944 | tf_op jit(solution)/shard_map/ppermute | solution.py:249
  53.2 2.5 %collective-permute-done.13.c2 = bf16[192,768]{1,0:T(8,128)(2,1)S(1)} collective-permute-done((bf16[192,768]{1,0:T(8,128)(2,1)S(1)}, bf16[192,768]{1,0:T(8,128)(2,1)S(1)}, u32[]{:S(2)}, u32[]{:S(2)}) %collective-permute-start.13) | collective-permute-done | bytes 294944 | tf_op jit(solution)/shard_map/ppermute | solution.py:249
  55.7 0.8 %finish.2.rest_0_ = bf16[256,768]{1,0:T(8,128)(2,1)} custom-call(f32[256,768]{1,0:T(8,128)S(1)} %get-tuple-element.35.own, bf16[192,768]{1,0:T(8,128)(2,1)S(1)} %collective-permute-done.12.c1, bf16[192,768]{1,0:T(8,128)(2,1)S(1)} %collective-permute-done.13.c2), custom_call_target="tpu_custom_call" | custom-call | flops 294912 | bytes 1474560 | tf_op jit(solution)/shard_map/finish/pallas_call | solution.py:203
  56.6 0.7 %finish.3 = bf16[256,768]{1,0:T(8,128)(2,1)} custom-call(f32[256,768]{1,0:T(8,128)S(1)} %get-tuple-element.35.own, bf16[64,768]{1,0:T(8,128)(2,1)S(1)} %collective-permute-done.10.c1, bf16[64,768]{1,0:T(8,128)(2,1)S(1)} %collective-permute-done.11.c2, bf16[256,768]{1,0:T(8,128)(2,1)} %finish.2.rest_0_), custom_call_target="tpu_custom_call", output_to_operand_aliasing={{}: (3, {})} | custom-call | flops 98304 | bytes 491520 | tf_op jit(solution)/shard_map/finish/pallas_call | solution.py:203
  (5 shorter events, 0.0 us)
Async XLA Ops:
  2.0 7.2 %collective-permute-start.5 = (bf16[256,768]{1,0:T(8,128)(2,1)S(1)}, bf16[256,768]{1,0:T(8,128)(2,1)S(1)}, u32[]{:S(2)}, u32[]{:S(2)}) collective-permute-start(bf16[256,768]{1,0:T(8,128)(2,1)S(1)} %get-tuple-element.32), channel_id=1, source_target_pairs={{0,240},{1,241},{2,242},{3,243},{4,244},{5,245},{6,246},{7,247},{8... | collective-permute-start | bytes 1179656 | tf_op jit(solution)/shard_map/ppermute | solution.py:249
  2.0 16.6 %collective-permute-start.2 = (bf16[256,768]{1,0:T(8,128)(2,1)S(1)}, bf16[256,768]{1,0:T(8,128)(2,1)S(1)}, u32[]{:S(2)}, u32[]{:S(2)}) collective-permute-start(bf16[256,768]{1,0:T(8,128)(2,1)S(1)} %get-tuple-element.26), channel_id=1, source_target_pairs={{0,24},{1,25},{2,26},{3,27},{4,28},{5,29},{6,30},{7,31},{8,16},{9,... | collective-permute-start | bytes 1179656 | tf_op jit(solution)/shard_map/ppermute | solution.py:249
  5.3 15.2 %collective-permute-start.1 = (bf16[256,768]{1,0:T(8,128)(2,1)S(1)}, bf16[256,768]{1,0:T(8,128)(2,1)S(1)}, u32[]{:S(2)}, u32[]{:S(2)}) collective-permute-start(bf16[256,768]{1,0:T(8,128)(2,1)S(1)} %get-tuple-element.26), channel_id=1, source_target_pairs={{0,17},{1,16},{2,19},{3,18},{4,21},{5,20},{6,23},{7,22},{8,25},{9,... | collective-permute-start | bytes 1179656 | tf_op jit(solution)/shard_map/ppermute | solution.py:249
  8.4 16.1 %collective-permute-start = (bf16[256,768]{1,0:T(8,128)(2,1)S(1)}, bf16[256,768]{1,0:T(8,128)(2,1)S(1)}, u32[]{:S(2)}, u32[]{:S(2)}) collective-permute-start(bf16[256,768]{1,0:T(8,128)(2,1)S(1)} %get-tuple-element.26), channel_id=1, source_target_pairs={{0,16},{1,17},{2,18},{3,19},{4,20},{5,21},{6,22},{7,23},{8,24},{9,... | collective-permute-start | bytes 1179656 | tf_op jit(solution)/shard_map/ppermute | solution.py:249
  8.8 18.8 %collective-permute-start.9 = (bf16[256,768]{1,0:T(8,128)(2,1)}, bf16[256,768]{1,0:T(8,128)(2,1)S(1)}, u32[]{:S(2)}, u32[]{:S(2)}) collective-permute-start(bf16[256,768]{1,0:T(8,128)(2,1)} %bitcast.18), channel_id=1, source_target_pairs={{0,8},{1,9},{2,10},{3,11},{4,12},{5,13},{6,14},{7,15},{8,0},{9,1},... | collective-permute-start | bytes 1179656 | tf_op jit(solution)/shard_map/ppermute | solution.py:249
  9.1 21.5 %collective-permute-start.8 = (bf16[256,768]{1,0:T(8,128)(2,1)}, bf16[256,768]{1,0:T(8,128)(2,1)S(1)}, u32[]{:S(2)}, u32[]{:S(2)}) collective-permute-start(bf16[256,768]{1,0:T(8,128)(2,1)} %bitcast.19), channel_id=1, source_target_pairs={{0,1},{1,0},{2,3},{3,2},{4,5},{5,4},{6,7},{7,6},{8,9},{9,8},{10,11... | collective-permute-start | bytes 1179656 | tf_op jit(solution)/shard_map/ppermute | solution.py:249
  18.6 14.1 %collective-permute-start.7 = (bf16[256,768]{1,0:T(8,128)(2,1)S(1)}, bf16[256,768]{1,0:T(8,128)(2,1)S(1)}, u32[]{:S(2)}, u32[]{:S(2)}) collective-permute-start(bf16[256,768]{1,0:T(8,128)(2,1)S(1)} %collective-permute-done.5.g0), channel_id=1, source_target_pairs={{0,8},{1,9},{2,10},{3,11},{4,12},{5,13},{6,14},{7,15},{8,0},{9,1},... | collective-permute-start | bytes 1179656 | tf_op jit(solution)/shard_map/ppermute | solution.py:249
  20.5 18.6 %collective-permute-start.6 = (bf16[256,768]{1,0:T(8,128)(2,1)S(1)}, bf16[256,768]{1,0:T(8,128)(2,1)S(1)}, u32[]{:S(2)}, u32[]{:S(2)}) collective-permute-start(bf16[256,768]{1,0:T(8,128)(2,1)S(1)} %collective-permute-done.5.g0), channel_id=1, source_target_pairs={{0,1},{1,0},{2,3},{3,2},{4,5},{5,4},{6,7},{7,6},{8,9},{9,8},{10,11... | collective-permute-start | bytes 1179656 | tf_op jit(solution)/shard_map/ppermute | solution.py:249
  27.0 20.5 %collective-permute-start.3 = (bf16[256,768]{1,0:T(8,128)(2,1)S(1)}, bf16[256,768]{1,0:T(8,128)(2,1)S(1)}, u32[]{:S(2)}, u32[]{:S(2)}) collective-permute-start(bf16[256,768]{1,0:T(8,128)(2,1)S(1)} %get-tuple-element.30), channel_id=1, source_target_pairs={{0,1},{1,0},{2,3},{3,2},{4,5},{5,4},{6,7},{7,6},{8,9},{9,8},{10,11... | collective-permute-start | bytes 1179656 | tf_op jit(solution)/shard_map/ppermute | solution.py:249
  27.6 20.4 %collective-permute-start.4 = (bf16[256,768]{1,0:T(8,128)(2,1)S(1)}, bf16[256,768]{1,0:T(8,128)(2,1)S(1)}, u32[]{:S(2)}, u32[]{:S(2)}) collective-permute-start(bf16[256,768]{1,0:T(8,128)(2,1)S(1)} %get-tuple-element.31), channel_id=1, source_target_pairs={{0,8},{1,9},{2,10},{3,11},{4,12},{5,13},{6,14},{7,15},{8,0},{9,1},... | collective-permute-start | bytes 1179656 | tf_op jit(solution)/shard_map/ppermute | solution.py:249
  41.6 15.0 %collective-permute-start.10 = (bf16[64,768]{1,0:T(8,128)(2,1)S(1)}, bf16[64,768]{1,0:T(8,128)(2,1)S(1)}, u32[]{:S(2)}, u32[]{:S(2)}) collective-permute-start(bf16[64,768]{1,0:T(8,128)(2,1)S(1)} %get-tuple-element.36), channel_id=1, source_target_pairs={{0,1},{1,0},{2,3},{3,2},{4,5},{5,4},{6,7},{7,6},{8,9},{9,8},{10,11... | collective-permute-start | bytes 294920 | tf_op jit(solution)/shard_map/ppermute | solution.py:249
  42.5 14.1 %collective-permute-start.11 = (bf16[64,768]{1,0:T(8,128)(2,1)S(1)}, bf16[64,768]{1,0:T(8,128)(2,1)S(1)}, u32[]{:S(2)}, u32[]{:S(2)}) collective-permute-start(bf16[64,768]{1,0:T(8,128)(2,1)S(1)} %get-tuple-element.37), channel_id=1, source_target_pairs={{0,8},{1,9},{2,10},{3,11},{4,12},{5,13},{6,14},{7,15},{8,0},{9,1},... | collective-permute-start | bytes 294920 | tf_op jit(solution)/shard_map/ppermute | solution.py:249
  42.8 10.4 %collective-permute-start.12 = (bf16[192,768]{1,0:T(8,128)(2,1)S(1)}, bf16[192,768]{1,0:T(8,128)(2,1)S(1)}, u32[]{:S(2)}, u32[]{:S(2)}) collective-permute-start(bf16[192,768]{1,0:T(8,128)(2,1)S(1)} %get-tuple-element.38), channel_id=1, source_target_pairs={{0,1},{1,0},{2,3},{3,2},{4,5},{5,4},{6,7},{7,6},{8,9},{9,8},{10,11... | collective-permute-start | bytes 884744 | tf_op jit(solution)/shard_map/ppermute | solution.py:249
  47.5 8.2 %collective-permute-start.13 = (bf16[192,768]{1,0:T(8,128)(2,1)S(1)}, bf16[192,768]{1,0:T(8,128)(2,1)S(1)}, u32[]{:S(2)}, u32[]{:S(2)}) collective-permute-start(bf16[192,768]{1,0:T(8,128)(2,1)S(1)} %get-tuple-element.39), channel_id=1, source_target_pairs={{0,8},{1,9},{2,10},{3,11},{4,12},{5,13},{6,14},{7,15},{8,0},{9,1},... | collective-permute-start | bytes 884744 | tf_op jit(solution)/shard_map/ppermute | solution.py:249

commit v2 on v0

--- a/solution.py
+++ b/solution.py
@@ -24,7 +24,8 @@
 
 
 def gelu(v):
-    return 0.5 * v * (1.0 + jnp.tanh(ROOT * (v + CUBE * v * v * v)))
+    half = 0.5 * v
+    return half + half * jnp.tanh(v * (ROOT + (ROOT * CUBE) * (v * v)))
 
 
 def gelu_and_slope(v):
@@ -47,15 +48,21 @@
 
 def forward_kernel(cin, cout, x0, x1, x2, w_in, w_out, own, c1, c2, acc):
     hidden, slots, size, _ = w_in.shape
+    sums = (own, acc.at[0], acc.at[1])
+
+    def value(h):
+        x = picked(cin, h, (x0, x1, x2), size)
+        return dot(x, w_in[h].reshape(slots * size, size), NN)
+
+    pre = value(0)
     own[...] = x0[...].astype(F32)
     acc[...] = jnp.zeros_like(acc)
-    sums = (own, acc.at[0], acc.at[1])
-    for h in range(hidden):
-        x = picked(cin, h, (x0, x1, x2), size)
-        pre = dot(x, w_in[h].reshape(slots * size, size), NN)
+    for h in range(hidden):
+        later = value(h + 1) if h + 1 < hidden else None
         hid = gelu(pre).astype(BF)
         for k in range(slots):
             sums[k][:, column(cout, h, k, size)] += dot(hid, w_out[h, k], NN)
+        pre = later
     c1[...] = acc[0].astype(BF)
     c2[...] = acc[1].astype(BF)
 

time: 55.1 us -> 55.1 us (level)
  no operation moved by 1% of the time
where the time goes in v2:
time: 55.1 us; the launch traced here: 55 us
  waiting for transfers between devices  22.1 us (40%)
  starting transfers between devices  16.3 us (30%)
  Pallas kernels  14.1 us (26%)
  other arithmetic  1.76 us (3%)
  between operations  0.7 us (1%)
    ppermute x12, waiting for transfers between devices, send(): return lax.ppermute(value, ('pipe', 'tensor'), route)  22.1 us
    ppermute x12, starting transfers between devices, send(): return lax.ppermute(value, ('pipe', 'tensor'), route)  16.3 us
    pallas_call x4, Pallas kernels, run(): pl.pallas_call(body, in_specs=[SMEM] * len(tables) + [VMEM] * len(ins), o...  10.4 us
    pallas_call x1, Pallas kernels, stage(): pl.pallas_call(stage_kernel, in_specs=[HBM] * 2, out_specs=(VMEM,) * 2, s...  2.4 us
    broadcast_in_dim x2, other arithmetic, shards(): return (out_acts[None], in_grads[None], gw_in[None], gw_out[None])  1.76 us
    pallas_call x1, Pallas kernels, pick(): pl.pallas_call(functools.partial(pick_kernel, lax.axis_size('pipe')), in_...  1.32 us
  transfers between devices with their start and end apart: 12, of which 8 were waited for; matrix products, arithmetic and copies ran while one was open for 2% of the time, Pallas kernels for 23%

profile of v2, /device:TPU:2, one launch (start us, length us, event | category | flops | bytes accessed | tf_op | source)
XLA Modules:
  0.0 55.0 jit_solution(11181476943009560899)
XLA Ops:
  0.6 1.3 %pick.1 = (bf16[256,768]{1,0:T(8,128)(2,1)S(1)}, bf16[256,768]{1,0:T(8,128)(2,1)S(1)}, bf16[256,768]{1,0:T(8,128)(2,1)S(1)}, s32[3,6]{1,0:T(4,128)S(1)}, s32[3,6]{1,0:T(4,128)S(1)}) custom-call(bf16[256,768]{1,0:T(8,128)(2,1)} %bitcast.15, bf16[256,768]{1,0:T(8,128)(2,1)} %first_a.1, bf16[256,768]{1,0:T(8,128)(2,1)} %bitcast.16, bf16[256,768]{1,0:T(8,128)(2,1)} %last_g.1, ...), custom_call_target="tpu_custom_call" | custom-call | bytes 2359296 | tf_op jit(solution)/shard_map/pick/pallas_call | solution.py:153
  2.0 5.3 %collective-permute-start.5 = (bf16[256,768]{1,0:T(8,128)(2,1)S(1)}, bf16[256,768]{1,0:T(8,128)(2,1)S(1)}, u32[]{:S(2)}, u32[]{:S(2)}) collective-permute-start(bf16[256,768]{1,0:T(8,128)(2,1)S(1)} %get-tuple-element.30), channel_id=1, source_target_pairs={{0,240},{1,241},{2,242},{3,243},{4,244},{5,245},{6,246},{7,247},{8... | collective-permute-start | bytes 1179656 | tf_op jit(solution)/shard_map/ppermute | solution.py:226
  7.3 0.0 collective-permute-start.2
  7.3 0.0 collective-permute-start.1
  7.3 0.0 collective-permute-start
  7.3 3.3 %collective-permute-start.9 = (bf16[256,768]{1,0:T(8,128)(2,1)}, bf16[256,768]{1,0:T(8,128)(2,1)S(1)}, u32[]{:S(2)}, u32[]{:S(2)}) collective-permute-start(bf16[256,768]{1,0:T(8,128)(2,1)} %bitcast.18), channel_id=1, source_target_pairs={{0,8},{1,9},{2,10},{3,11},{4,12},{5,13},{6,14},{7,15},{8,0},{9,1},... | collective-permute-start | bytes 1179656 | tf_op jit(solution)/shard_map/ppermute | solution.py:226
  10.6 2.0 %collective-permute-done.5.g0 = bf16[256,768]{1,0:T(8,128)(2,1)S(1)} collective-permute-done((bf16[256,768]{1,0:T(8,128)(2,1)S(1)}, bf16[256,768]{1,0:T(8,128)(2,1)S(1)}, u32[]{:S(2)}, u32[]{:S(2)}) %collective-permute-start.5) | collective-permute-done | bytes 393248 | tf_op jit(solution)/shard_map/ppermute | solution.py:226
  12.6 0.5 collective-permute-start.8
  13.1 6.7 %collective-permute-done.2.x2 = bf16[256,768]{1,0:T(8,128)(2,1)S(1)} collective-permute-done((bf16[256,768]{1,0:T(8,128)(2,1)S(1)}, bf16[256,768]{1,0:T(8,128)(2,1)S(1)}, u32[]{:S(2)}, u32[]{:S(2)}) %collective-permute-start.2) | collective-permute-done | bytes 393248 | tf_op jit(solution)/shard_map/ppermute | solution.py:226
  19.8 3.2 %collective-permute-start.7 = (bf16[256,768]{1,0:T(8,128)(2,1)S(1)}, bf16[256,768]{1,0:T(8,128)(2,1)S(1)}, u32[]{:S(2)}, u32[]{:S(2)}) collective-permute-start(bf16[256,768]{1,0:T(8,128)(2,1)S(1)} %collective-permute-done.5.g0), channel_id=1, source_target_pairs={{0,8},{1,9},{2,10},{3,11},{4,12},{5,13},{6,14},{7,15},{8,0},{9,1},... | collective-permute-start | bytes 1179656 | tf_op jit(solution)/shard_map/ppermute | solution.py:226
  23.0 0.0 collective-permute-done.1.x1
  23.0 1.1 %collective-permute-start.6 = (bf16[256,768]{1,0:T(8,128)(2,1)S(1)}, bf16[256,768]{1,0:T(8,128)(2,1)S(1)}, u32[]{:S(2)}, u32[]{:S(2)}) collective-permute-start(bf16[256,768]{1,0:T(8,128)(2,1)S(1)} %collective-permute-done.5.g0), channel_id=1, source_target_pairs={{0,1},{1,0},{2,3},{3,2},{4,5},{5,4},{6,7},{7,6},{8,9},{9,8},{10,11... | collective-permute-start | bytes 1179656 | tf_op jit(solution)/shard_map/ppermute | solution.py:226
  24.1 2.4 %stage.1 = (bf16[6,3,256,256]{3,2,1,0:T(8,128)(2,1)S(1)}, bf16[6,3,256,256]{3,2,1,0:T(8,128)(2,1)S(1)}) custom-call(bf16[6,3,256,256]{3,2,1,0:T(8,128)(2,1)} %bitcast.13, bf16[6,3,256,256]{3,2,1,0:T(8,128)(2,1)} %bitcast.14), custom_call_target="tpu_custom_call" | custom-call | bytes 9437184 | tf_op jit(solution)/shard_map/stage/pallas_call | solution.py:181
  26.5 0.3 collective-permute-done.x0
  26.8 2.5 %shard_map.120 = (f32[256,768]{1,0:T(8,128)S(1)}, bf16[256,768]{1,0:T(8,128)(2,1)S(1)}, bf16[256,768]{1,0:T(8,128)(2,1)S(1)}) custom-call(s32[3,6]{1,0:T(4,128)S(1)} %get-tuple-element.22.cin, s32[3,6]{1,0:T(4,128)S(1)} %get-tuple-element.23.cout, bf16[256,768]{1,0:T(8,128)(2,1)S(1)} %collective-permute-done.x0, ...), custom_call_target="tpu_custom_call" | custom-call | flops 1207959552 | bytes 7471104 | tf_op jit(solution)/shard_map/pallas_call | solution.py:199
  29.3 0.7 %collective-permute-start.3 = (bf16[256,768]{1,0:T(8,128)(2,1)S(1)}, bf16[256,768]{1,0:T(8,128)(2,1)S(1)}, u32[]{:S(2)}, u32[]{:S(2)}) collective-permute-start(bf16[256,768]{1,0:T(8,128)(2,1)S(1)} %get-tuple-element.28), channel_id=1, source_target_pairs={{0,1},{1,0},{2,3},{3,2},{4,5},{5,4},{6,7},{7,6},{8,9},{9,8},{10,11... | collective-permute-start | bytes 1179656 | tf_op jit(solution)/shard_map/ppermute | solution.py:226
  30.1 0.3 collective-permute-done.9.x2
  30.4 0.0 collective-permute-start.4
  30.4 0.0 collective-permute-done.8.x1
  30.4 2.0 %shard_map.121 = (bf16[256,1536]{1,0:T(8,128)(2,1)S(1)}, f32[256,1536]{1,0:T(8,128)S(1)}) custom-call(s32[3,6]{1,0:T(4,128)S(1)} %get-tuple-element.22.cin, bf16[256,768]{1,0:T(8,128)(2,1)S(1)} %get-tuple-element.31.x0, bf16[256,768]{1,0:T(8,128)(2,1)S(1)} %collective-permute-done.8.x1, bf16[256,768]{1,0:T(8,128)(2,1)S(1)} %collective-permute-done.9.x2, ...), custom_call_target="tpu_custom_call" | custom-call | flops 603979776 | bytes 5898240 | tf_op jit(solution)/shard_map/pallas_call | solution.py:199
  32.4 6.4 %collective-permute-done.7.g2 = bf16[256,768]{1,0:T(8,128)(2,1)S(1)} collective-permute-done((bf16[256,768]{1,0:T(8,128)(2,1)S(1)}, bf16[256,768]{1,0:T(8,128)(2,1)S(1)}, u32[]{:S(2)}, u32[]{:S(2)}) %collective-permute-start.7) | collective-permute-done | bytes 393248 | tf_op jit(solution)/shard_map/ppermute | solution.py:226
  38.8 0.0 collective-permute-done.6.g1
  38.8 2.6 %shard_map.122 = (f32[256,768]{1,0:T(8,128)S(1)}, bf16[256,768]{1,0:T(8,128)(2,1)S(1)}, bf16[256,768]{1,0:T(8,128)(2,1)S(1)}, bf16[256,1536]{1,0:T(8,128)(2,1)S(1)}) custom-call(s32[3,6]{1,0:T(4,128)S(1)} %get-tuple-element.22.cin, s32[3,6]{1,0:T(4,128)S(1)} %get-tuple-element.23.cout, bf16[256,768]{1,0:T(8,128)(2,1)S(1)} %collective-permute-done.5.g0, ...), custom_call_target="tpu_custom_call" | custom-call | flops 1207959552 | bytes 9830400 | tf_op jit(solution)/shard_map/pallas_call | solution.py:199
  41.4 1.1 %collective-permute-start.10 = (bf16[256,768]{1,0:T(8,128)(2,1)S(1)}, bf16[256,768]{1,0:T(8,128)(2,1)S(1)}, u32[]{:S(2)}, u32[]{:S(2)}) collective-permute-start(bf16[256,768]{1,0:T(8,128)(2,1)S(1)} %get-tuple-element.34), channel_id=1, source_target_pairs={{0,1},{1,0},{2,3},{3,2},{4,5},{5,4},{6,7},{7,6},{8,9},{9,8},{10,11... | collective-permute-start | bytes 1179656 | tf_op jit(solution)/shard_map/ppermute | solution.py:226
  42.4 1.0 %collective-permute-start.11 = (bf16[256,768]{1,0:T(8,128)(2,1)S(1)}, bf16[256,768]{1,0:T(8,128)(2,1)S(1)}, u32[]{:S(2)}, u32[]{:S(2)}) collective-permute-start(bf16[256,768]{1,0:T(8,128)(2,1)S(1)} %get-tuple-element.35), channel_id=1, source_target_pairs={{0,8},{1,9},{2,10},{3,11},{4,12},{5,13},{6,14},{7,15},{8,0},{9,1},... | collective-permute-start | bytes 1179656 | tf_op jit(solution)/shard_map/ppermute | solution.py:226
  43.5 3.3 %shard_map.123 = (bf16[6,3,256,256]{3,2,1,0:T(8,128)(2,1)}, bf16[6,3,256,256]{3,2,1,0:T(8,128)(2,1)}) custom-call(s32[3,6]{1,0:T(4,128)S(1)} %get-tuple-element.22.cin, s32[3,6]{1,0:T(4,128)S(1)} %get-tuple-element.23.cout, bf16[256,768]{1,0:T(8,128)(2,1)S(1)} %get-tuple-element.31.x0, bf16[256,768]{1,0:T(8,128)(2,1)S(1)} %collective-permute-done.8.x1, ...), custom_call_target="tpu_custom_call" | custom-call | flops 1207959552 | bytes 8650752 | tf_op jit(solution)/shard_map/pallas_call | solution.py:199
  46.8 0.0 collective-permute-done.3
  46.8 0.4 collective-permute-done.4
  47.2 0.9 %fusion = bf16[1,256,768]{2,1,0:T(8,128)(2,1)} fusion(bf16[256,768]{1,0:T(8,128)(2,1)S(1)} %collective-permute-done.4, f32[256,768]{1,0:T(8,128)S(1)} %get-tuple-element.27, bf16[256,768]{1,0:T(8,128)(2,1)S(1)} %collective-permute-done.3), kind=kLoop, calls=%fused_computation.2 | loop fusion | flops 983040 | bytes 1966080 | tf_op jit(solution)/shard_map/broadcast_in_dim | solution.py:273
  48.1 3.9 %collective-permute-done.10 = bf16[256,768]{1,0:T(8,128)(2,1)S(1)} collective-permute-done((bf16[256,768]{1,0:T(8,128)(2,1)S(1)}, bf16[256,768]{1,0:T(8,128)(2,1)S(1)}, u32[]{:S(2)}, u32[]{:S(2)}) %collective-permute-start.10) | collective-permute-done | bytes 393248 | tf_op jit(solution)/shard_map/ppermute | solution.py:226
  52.0 2.1 %collective-permute-done.11 = bf16[256,768]{1,0:T(8,128)(2,1)S(1)} collective-permute-done((bf16[256,768]{1,0:T(8,128)(2,1)S(1)}, bf16[256,768]{1,0:T(8,128)(2,1)S(1)}, u32[]{:S(2)}, u32[]{:S(2)}) %collective-permute-start.11) | collective-permute-done | bytes 393248 | tf_op jit(solution)/shard_map/ppermute | solution.py:226
  54.1 0.9 %fusion.1 = bf16[1,256,768]{2,1,0:T(8,128)(2,1)} fusion(bf16[256,768]{1,0:T(8,128)(2,1)S(1)} %collective-permute-done.11, f32[256,768]{1,0:T(8,128)S(1)} %get-tuple-element.33, bf16[256,768]{1,0:T(8,128)(2,1)S(1)} %collective-permute-done.10), kind=kLoop, calls=%fused_computation.3 | loop fusion | flops 983040 | bytes 1966080 | tf_op jit(solution)/shard_map/broadcast_in_dim | solution.py:273
Async XLA Ops:
  2.0 10.6 %collective-permute-start.5 = (bf16[256,768]{1,0:T(8,128)(2,1)S(1)}, bf16[256,768]{1,0:T(8,128)(2,1)S(1)}, u32[]{:S(2)}, u32[]{:S(2)}) collective-permute-start(bf16[256,768]{1,0:T(8,128)(2,1)S(1)} %get-tuple-element.30), channel_id=1, source_target_pairs={{0,240},{1,241},{2,242},{3,243},{4,244},{5,245},{6,246},{7,247},{8... | collective-permute-start | bytes 1179656 | tf_op jit(solution)/shard_map/ppermute | solution.py:226
  7.3 12.5 %collective-permute-start.2 = (bf16[256,768]{1,0:T(8,128)(2,1)S(1)}, bf16[256,768]{1,0:T(8,128)(2,1)S(1)}, u32[]{:S(2)}, u32[]{:S(2)}) collective-permute-start(bf16[256,768]{1,0:T(8,128)(2,1)S(1)} %get-tuple-element.24), channel_id=1, source_target_pairs={{0,24},{1,25},{2,26},{3,27},{4,28},{5,29},{6,30},{7,31},{8,16},{9,... | collective-permute-start | bytes 1179656 | tf_op jit(solution)/shard_map/ppermute | solution.py:226
  7.3 15.7 %collective-permute-start.1 = (bf16[256,768]{1,0:T(8,128)(2,1)S(1)}, bf16[256,768]{1,0:T(8,128)(2,1)S(1)}, u32[]{:S(2)}, u32[]{:S(2)}) collective-permute-start(bf16[256,768]{1,0:T(8,128)(2,1)S(1)} %get-tuple-element.24), channel_id=1, source_target_pairs={{0,17},{1,16},{2,19},{3,18},{4,21},{5,20},{6,23},{7,22},{8,25},{9,... | collective-permute-start | bytes 1179656 | tf_op jit(solution)/shard_map/ppermute | solution.py:226
  7.3 19.5 %collective-permute-start = (bf16[256,768]{1,0:T(8,128)(2,1)S(1)}, bf16[256,768]{1,0:T(8,128)(2,1)S(1)}, u32[]{:S(2)}, u32[]{:S(2)}) collective-permute-start(bf16[256,768]{1,0:T(8,128)(2,1)S(1)} %get-tuple-element.24), channel_id=1, source_target_pairs={{0,16},{1,17},{2,18},{3,19},{4,20},{5,21},{6,22},{7,23},{8,24},{9,... | collective-permute-start | bytes 1179656 | tf_op jit(solution)/shard_map/ppermute | solution.py:226
  7.3 23.1 %collective-permute-start.9 = (bf16[256,768]{1,0:T(8,128)(2,1)}, bf16[256,768]{1,0:T(8,128)(2,1)S(1)}, u32[]{:S(2)}, u32[]{:S(2)}) collective-permute-start(bf16[256,768]{1,0:T(8,128)(2,1)} %bitcast.18), channel_id=1, source_target_pairs={{0,8},{1,9},{2,10},{3,11},{4,12},{5,13},{6,14},{7,15},{8,0},{9,1},... | collective-permute-start | bytes 1179656 | tf_op jit(solution)/shard_map/ppermute | solution.py:226
  12.6 17.8 %collective-permute-start.8 = (bf16[256,768]{1,0:T(8,128)(2,1)}, bf16[256,768]{1,0:T(8,128)(2,1)S(1)}, u32[]{:S(2)}, u32[]{:S(2)}) collective-permute-start(bf16[256,768]{1,0:T(8,128)(2,1)} %bitcast.19), channel_id=1, source_target_pairs={{0,1},{1,0},{2,3},{3,2},{4,5},{5,4},{6,7},{7,6},{8,9},{9,8},{10,11... | collective-permute-start | bytes 1179656 | tf_op jit(solution)/shard_map/ppermute | solution.py:226
  19.8 19.0 %collective-permute-start.7 = (bf16[256,768]{1,0:T(8,128)(2,1)S(1)}, bf16[256,768]{1,0:T(8,128)(2,1)S(1)}, u32[]{:S(2)}, u32[]{:S(2)}) collective-permute-start(bf16[256,768]{1,0:T(8,128)(2,1)S(1)} %collective-permute-done.5.g0), channel_id=1, source_target_pairs={{0,8},{1,9},{2,10},{3,11},{4,12},{5,13},{6,14},{7,15},{8,0},{9,1},... | collective-permute-start | bytes 1179656 | tf_op jit(solution)/shard_map/ppermute | solution.py:226
  23.0 15.8 %collective-permute-start.6 = (bf16[256,768]{1,0:T(8,128)(2,1)S(1)}, bf16[256,768]{1,0:T(8,128)(2,1)S(1)}, u32[]{:S(2)}, u32[]{:S(2)}) collective-permute-start(bf16[256,768]{1,0:T(8,128)(2,1)S(1)} %collective-permute-done.5.g0), channel_id=1, source_target_pairs={{0,1},{1,0},{2,3},{3,2},{4,5},{5,4},{6,7},{7,6},{8,9},{9,8},{10,11... | collective-permute-start | bytes 1179656 | tf_op jit(solution)/shard_map/ppermute | solution.py:226
  29.3 17.4 %collective-permute-start.3 = (bf16[256,768]{1,0:T(8,128)(2,1)S(1)}, bf16[256,768]{1,0:T(8,128)(2,1)S(1)}, u32[]{:S(2)}, u32[]{:S(2)}) collective-permute-start(bf16[256,768]{1,0:T(8,128)(2,1)S(1)} %get-tuple-element.28), channel_id=1, source_target_pairs={{0,1},{1,0},{2,3},{3,2},{4,5},{5,4},{6,7},{7,6},{8,9},{9,8},{10,11... | collective-permute-start | bytes 1179656 | tf_op jit(solution)/shard_map/ppermute | solution.py:226
  30.4 16.9 %collective-permute-start.4 = (bf16[256,768]{1,0:T(8,128)(2,1)S(1)}, bf16[256,768]{1,0:T(8,128)(2,1)S(1)}, u32[]{:S(2)}, u32[]{:S(2)}) collective-permute-start(bf16[256,768]{1,0:T(8,128)(2,1)S(1)} %get-tuple-element.29), channel_id=1, source_target_pairs={{0,8},{1,9},{2,10},{3,11},{4,12},{5,13},{6,14},{7,15},{8,0},{9,1},... | collective-permute-start | bytes 1179656 | tf_op jit(solution)/shard_map/ppermute | solution.py:226
  41.4 10.7 %collective-permute-start.10 = (bf16[256,768]{1,0:T(8,128)(2,1)S(1)}, bf16[256,768]{1,0:T(8,128)(2,1)S(1)}, u32[]{:S(2)}, u32[]{:S(2)}) collective-permute-start(bf16[256,768]{1,0:T(8,128)(2,1)S(1)} %get-tuple-element.34), channel_id=1, source_target_pairs={{0,1},{1,0},{2,3},{3,2},{4,5},{5,4},{6,7},{7,6},{8,9},{9,8},{10,11... | collective-permute-start | bytes 1179656 | tf_op jit(solution)/shard_map/ppermute | solution.py:226
  42.4 11.7 %collective-permute-start.11 = (bf16[256,768]{1,0:T(8,128)(2,1)S(1)}, bf16[256,768]{1,0:T(8,128)(2,1)S(1)}, u32[]{:S(2)}, u32[]{:S(2)}) collective-permute-start(bf16[256,768]{1,0:T(8,128)(2,1)S(1)} %get-tuple-element.35), channel_id=1, source_target_pairs={{0,8},{1,9},{2,10},{3,11},{4,12},{5,13},{6,14},{7,15},{8,0},{9,1},... | collective-permute-start | bytes 1179656 | tf_op jit(solution)/shard_map/ppermute | solution.py:226
